TPU v7x, 128 devices: a whole 4x4x4 slice. The times are simulated.
128 devices in a mesh: group: 4 (over y_lo, core), mp: 32 (over z, x, y_hi).
Axes of the slice: x: 4, y: 4 (y_hi: 2, y_lo: 2; y = y_hi * 2 + y_lo), z: 4, core: 2. Of those that a mesh axis runs over, the one named last changes fastest.
Arguments:
- tokens: bfloat16 [5120, 2048], P(('group', 'mp')), may hold values from -6 to 6
- lengths: int32 [4, 8], P('group'), may hold values from 1 to 512, 1280 in all within a row
- query_gain: float32 [2048], replicated, may hold values from 0.5 to 8
- key_gain: float32 [2048], replicated, may hold values from 0.5 to 8
- attn_post_gain: float32 [2048], replicated, may hold values from 0.5 to 1.5
- mlp_post_gain: float32 [2048], replicated, may hold values from 0.5 to 1.5
- query_weight: float32 [2048, 2048], P(('mp', 'group')), may hold values from -4 to 4
- key_weight: float32 [2048, 2048], P(('mp', 'group')), may hold values from -4 to 4
- value_weight: float32 [2048, 2048], P(('mp', 'group')), may hold values from -0.125 to 0.125
- output_weight: float32 [2048, 2048], P(('mp', 'group')), may hold values from -0.125 to 0.125
- gate_weight: float32 [2048, 8192], P(('mp', 'group')), may hold values from -0.125 to 0.125
- up_weight: float32 [2048, 8192], P(('mp', 'group')), may hold values from -0.125 to 0.125
- down_weight: float32 [8192, 2048], P(('mp', 'group')), may hold values from -0.0625 to 0.0625
Outputs:
- layer_out: bfloat16 [5120, 2048], P(('group', 'mp'))
Inputs may be any that keep to these rules, and one draw needn't show every extreme that they name: In each group the 8 prompt lengths sum to 1280; the longest is exactly 512.
All inputs are finite; a program needn't handle non-finite values.
Results may differ from a plain program's by a relative error of at most 0.034.
Values may be sent and summed in bfloat16 or wider, within the bound.
A program may use at most 64 MiB of HBM per device.

v0:
```python
import math
import jax
import jax.numpy as jnp
from jax import lax
from jax.sharding import PartitionSpec as P

HEAD_DIM = 128
NORM_EPSILON = 1e-06
ROPE_BASE = 500000.0


def partner_2(block, axis, apart):
    count = lax.axis_size(axis)
    route = []
    for low in range(count):
        high = low | 1 << apart
        if high != low and high < count:
            route += [(low, high), (high, low)]
    return lax.ppermute(block, axis, route)


def token_layout(prompt_lens, row_count):
    seg_ends = jnp.cumsum(prompt_lens)
    starts = seg_ends - prompt_lens
    indices = jnp.arange(row_count, dtype=jnp.int32)
    segment = jnp.sum((indices[:, None] >= seg_ends[None, :]).astype(jnp.int32), axis=1)
    member = segment[:, None] == jnp.arange(prompt_lens.shape[0], dtype=jnp.int32)[None, :]
    opening = jnp.sum(jnp.where(member, starts[None, :], 0), axis=1)
    return (segment, indices - opening)


def rotary(head_values, position, head_size):
    half_size = head_size // 2
    frequency = jnp.exp(
        jnp.arange(half_size, dtype=jnp.float32) * (-2.0 * math.log(ROPE_BASE) / head_size)
    )
    angles = position.astype(jnp.float32)[:, None] * frequency[None, :]
    cosines = jnp.cos(angles)
    sines = jnp.sin(angles)
    front_half = head_values[..., :half_size]
    back_half = head_values[..., half_size:]
    return jnp.concatenate(
        [front_half * cosines - back_half * sines, back_half * cosines + front_half * sines],
        axis=-1,
    )


def head_attention(queries, query_rows, keys_rot, values_h, segment, head_size):
    scores = lax.dot_general(
        queries, keys_rot, (((1,), (1,)), ((), ())), preferred_element_type=jnp.float32
    )
    scores = scores * (1.0 / math.sqrt(head_size))
    key_rows = jnp.arange(keys_rot.shape[0], dtype=jnp.int32)
    query_segment = jnp.take(segment, query_rows)
    allowed = (query_segment[:, None] == segment[None, :]) & (
        key_rows[None, :] <= query_rows[:, None]
    )
    scores = jnp.where(allowed, scores, -1e30)
    row_max = jnp.max(scores, axis=1, keepdims=True)
    weights = jnp.exp(scores - row_max)
    weights = weights / jnp.sum(weights, axis=1, keepdims=True)
    probabilities = weights.astype(jnp.bfloat16)
    return jnp.dot(probabilities, values_h, preferred_element_type=jnp.float32).astype(jnp.bfloat16)


def rms_scale(values_in, gain):
    return (
        values_in
        * lax.rsqrt(jnp.mean(values_in * values_in, axis=-1, keepdims=True) + NORM_EPSILON)
        * gain
    )


def per_device(
    tokens,
    lengths,
    query_gain,
    key_gain,
    attn_post_gain,
    mlp_post_gain,
    query_weight,
    key_weight,
    value_weight,
    output_weight,
    gate_weight,
    up_weight,
    down_weight,
):
    features = tokens.shape[1]
    shards = lax.axis_size("mp")
    my_index = lax.axis_index("mp")
    col_width = features // shards
    tok_rows = tokens.shape[0]
    group_rows = tok_rows * shards
    stack_attn = jnp.stack([query_weight, key_weight, value_weight]).astype(jnp.bfloat16)
    stack_mlp = jnp.stack([gate_weight, up_weight]).astype(jnp.bfloat16)
    down_piece = down_weight.astype(jnp.bfloat16)[None]
    output_piece = output_weight.astype(jnp.bfloat16)[None]
    attn_rows, mlp_rows, down_rows, output_rows = (
        lax.all_gather(stack_attn, "group", axis=1, tiled=True),
        lax.all_gather(stack_mlp, "group", axis=1, tiled=True),
        lax.all_gather(down_piece, "group", axis=1, tiled=True),
        lax.all_gather(output_piece, "group", axis=1, tiled=True),
    )
    attn_block, mlp_block = (
        lax.all_to_all(attn_rows, "mp", split_axis=2, concat_axis=1, tiled=True),
        lax.all_to_all(mlp_rows, "mp", split_axis=2, concat_axis=1, tiled=True),
    )
    down_block = down_rows[0]
    output_block = output_rows[0]
    parity = my_index % 2
    partner = partner_2(attn_block, "mp", 0)
    attn_block = jnp.where(
        parity == 0,
        jnp.concatenate([attn_block, partner], axis=2),
        jnp.concatenate([partner, attn_block], axis=2),
    )
    head_cols = attn_block.shape[2]
    col_start = my_index * col_width // HEAD_DIM * HEAD_DIM
    share_part = col_width / head_cols
    projected = jnp.einsum(
        "td,kdc->ktc",
        lax.all_gather(tokens, "mp", axis=0, tiled=True),
        attn_block,
        preferred_element_type=jnp.float32,
    )
    query_sq = jnp.sum(projected[0] * projected[0], axis=1) * share_part
    key_sq = jnp.sum(projected[1] * projected[1], axis=1) * share_part
    query_total, key_total = lax.psum((query_sq, key_sq), "mp")
    query_part = lax.dynamic_slice_in_dim(query_gain, col_start, head_cols)
    key_part = lax.dynamic_slice_in_dim(key_gain, col_start, head_cols)
    q_normed = projected[0] * lax.rsqrt(query_total / features + NORM_EPSILON)[:, None] * query_part
    k_normed = projected[1] * lax.rsqrt(key_total / features + NORM_EPSILON)[:, None] * key_part
    segment, position = token_layout(lengths[0], group_rows)
    local_heads = head_cols // HEAD_DIM

    def heads_first(flat):
        return flat.reshape(group_rows, local_heads, HEAD_DIM).transpose(1, 0, 2)

    queries = rotary(heads_first(q_normed), position, HEAD_DIM).astype(jnp.bfloat16)
    keys_rot = rotary(heads_first(k_normed), position, HEAD_DIM).astype(jnp.bfloat16)
    values_h = heads_first(projected[2].astype(jnp.bfloat16))
    all_rows = jnp.arange(group_rows, dtype=jnp.int32)

    def per_head(triple):
        return head_attention(triple[0], all_rows, triple[1], triple[2], segment, HEAD_DIM)

    attended = lax.map(per_head, (queries, keys_rot, values_h))
    attended = attended.transpose(1, 0, 2).reshape(group_rows, head_cols)
    attended = lax.dynamic_slice_in_dim(attended, parity * col_width, col_width, 1)
    rows_part = attended
    attn_out = lax.psum_scatter(
        jnp.dot(rows_part, output_block, preferred_element_type=jnp.float32).astype(jnp.bfloat16),
        "mp",
        scatter_dimension=0,
        tiled=True,
    ).astype(jnp.float32)
    hidden = (tokens.astype(jnp.float32) + rms_scale(attn_out, attn_post_gain)).astype(jnp.bfloat16)
    hidden_width = mlp_block.shape[2]
    mlp_weights = jnp.concatenate([mlp_block[0], mlp_block[1]], axis=1)
    both_proj = jnp.dot(
        lax.all_gather(hidden, "mp", axis=0, tiled=True),
        mlp_weights,
        preferred_element_type=jnp.float32,
    )
    activated = (jax.nn.silu(both_proj[:, :hidden_width]) * both_proj[:, hidden_width:]).astype(
        jnp.bfloat16
    )
    rows_part = activated
    mlp_out = lax.psum_scatter(
        jnp.dot(rows_part, down_block, preferred_element_type=jnp.float32).astype(jnp.bfloat16),
        "mp",
        scatter_dimension=0,
        tiled=True,
    ).astype(jnp.float32)
    return (hidden.astype(jnp.float32) + rms_scale(mlp_out, mlp_post_gain)).astype(jnp.bfloat16)


def solution(mesh):
    return jax.shard_map(
        per_device,
        mesh=mesh,
        in_specs=(
            P(("group", "mp"), None),
            P("group", None),
            P(),
            P(),
            P(),
            P(),
            P(("mp", "group"), None),
            P(("mp", "group"), None),
            P(("mp", "group"), None),
            P(("mp", "group"), None),
            P(("mp", "group"), None),
            P(("mp", "group"), None),
            P(("mp", "group"), None),
        ),
        out_specs=P(("group", "mp"), None),
        check_vma=False,
    )
```

profile of v0, /device:TPU:0, one launch (start us, length us, event | category | flops | bytes accessed | tf_op | source)
XLA Modules:
  0.0 826.0 jit_solution(16544474879725775960)
XLA Ops:
  10.0 8.8 %all_gather.18 = bf16[3,64,2048]{2,1,0:T(8,128)(2,1)S(1)} all-gather(bf16[3,16,2048]{2,1,0:T(8,128)(2,1)S(1)} %pad_maximum_fusion.1), channel_id=1, replica_groups=mesh['group'=4,'mp'=32] {'group'}, dimensions={1}, use_global_device_ids=true | all-gather | bytes 983040 | tf_op jit(solution)/shard_map/all_gather | solution.py:100
  18.8 1.4 copy.34
  20.2 2.5 reshape.221
  22.6 10.5 %all-to-all-start = ((bf16[32,2,6144]{2,1,0:T(2,128)(2,1)}), bf16[32,2,6144]{2,1,0:T(2,128)(2,1)S(1)}, u32[]{:S(2)}, u32[]{:S(2)}) async-start(bf16[32,2,6144]{2,1,0:T(2,128)(2,1)} %reshape.221), calls=%async_computation | async-start | bytes 1572864 | tf_op jit(solution)/shard_map/all_to_all | solution.py:106
  35.0 7.1 gather_fusion
  42.1 5.8 all-gather
  47.9 2.3 all-to-all-done
  50.3 1.3 reshape.222
  51.6 2.5 copy.35
  54.1 2.8 all_to_all.27
  58.0 20.9 %collective-permute-done = bf16[3,2048,64]{1,2,0:T(8,128)(2,1)S(1)} collective-permute-done((bf16[3,2048,64]{1,2,0:T(8,128)(2,1)S(1)}, bf16[3,2048,64]{1,2,0:T(8,128)(2,1)S(1)}, u32[]{:S(2)}, u32[]{:S(2)}) %collective-permute-start) | collective-permute-done | bytes 786464 | tf_op jit(solution)/shard_map/ppermute | solution.py:19
  79.9 24.5 %all-gather.7.cloned.1.call-done = bf16[1280,2048]{1,0:T(8,128)(2,1)} async-done(((bf16[40,2048]{1,0:T(8,128)(2,1)}), bf16[1280,2048]{1,0:T(8,128)(2,1)}) %all-gather.7.cloned.1.call-update) | async-done | bytes 5242896 | tf_op jit(solution)/shard_map/all_gather | solution.py:123
  104.3 5.2 fusion.6
  109.7 181.7 %all-reduce = (f32[1280]{0:T(1024)S(1)}, f32[1280]{0:T(1024)S(1)}) all-reduce(f32[1280]{0:T(1024)S(1)} %broadcast_multiply_fusion.1, f32[1280]{0:T(1024)S(1)} %broadcast_multiply_fusion), channel_id=1, replica_groups=mesh['group'=4,'mp'=32] {'mp'}, use_global_device_ids=true, to_apply=%region_3.4 | all-reduce | flops 2560 | bytes 20480 | tf_op jit(solution)/shard_map/psum | solution.py:129
  291.6 1.5 fusion.55
  293.1 1.5 fusion.66
  295.6 1.3 fusion.5
  296.9 3.9 convolution_convert_fusion.1
  303.0 195.8 %reduce-scatter.3.cloned.1.call-done = bf16[40,2048]{1,0:T(8,128)(2,1)} async-done(((bf16[1280,2048]{1,0:T(8,128)(2,1)}), bf16[40,2048]{1,0:T(8,128)(2,1)}) %reduce-scatter.3.cloned.1.call-update) | async-done | bytes 163856 | tf_op jit(solution)/shard_map/reduce_scatter | solution.py:152
  499.8 1.7 fusion.33
  501.6 9.6 %copy.36 = bf16[2,64,8192]{1,0,2:T(2,128)(2,1)} copy(bf16[2,64,8192]{2,1,0:T(8,128)(2,1)} %all-gather.11.cloned.1.call-done) | data formatting | bytes 4194304 | tf_op jit(solution)/shard_map/all_gather | solution.py:101
  511.1 9.8 %reshape.223 = bf16[32,2,16384]{2,1,0:T(2,128)(2,1)} reshape(bf16[8192,2,64]{2,1,0:T(2,128)(2,1)} %bitcast.54) | data formatting | bytes 4194304
  521.0 4.9 all-to-all-start.1
  527.0 22.9 %all-to-all-done.1 = bf16[32,2,16384]{2,1,0:T(2,128)(2,1)S(1)} async-done(((bf16[32,2,16384]{2,1,0:T(2,128)(2,1)}), bf16[32,2,16384]{2,1,0:T(2,128)(2,1)S(1)}, u32[]{:S(2)}, u32[]{:S(2)}) %all-to-all-start.1) | async-done | bytes 2097184 | tf_op jit(solution)/shard_map/all_to_all | solution.py:107
  549.9 4.0 reshape.224
  554.0 6.4 copy.40
  561.7 32.2 %all-gather.9.cloned.1.call-done = bf16[1280,2048]{1,0:T(8,128)(2,1)} async-done(((bf16[40,2048]{1,0:T(8,128)(2,1)}), bf16[1280,2048]{1,0:T(8,128)(2,1)}) %all-gather.9.cloned.1.call-update) | async-done | bytes 5242896 | tf_op jit(solution)/shard_map/all_gather | solution.py:162
  593.9 6.9 fusion.9
  600.7 12.4 %all-gather.13.cloned.1.call-done = bf16[256,2048]{1,0:T(8,128)(2,1)} async-done(((bf16[64,2048]{1,0:T(8,128)(2,1)}), bf16[256,2048]{1,0:T(8,128)(2,1)}) %all-gather.13.cloned.1.call-update) | async-done | bytes 1048592 | tf_op jit(solution)/shard_map/all_gather | solution.py:102
  613.2 5.9 convolution_convert_fusion
  619.1 196.5 %reduce-scatter.5.cloned.1.call-done = bf16[40,2048]{1,0:T(8,128)(2,1)} async-done(((bf16[1280,2048]{1,0:T(8,128)(2,1)}), bf16[40,2048]{1,0:T(8,128)(2,1)}) %reduce-scatter.5.cloned.1.call-update) | async-done | bytes 163856 | tf_op jit(solution)/shard_map/reduce_scatter | solution.py:170
  816.6 1.7 fusion.37
  (66 shorter events, 14.6 us)
Async XLA Ops:
  7.4 97.0 %all-gather.7.cloned.1.call-start = ((), (), s32[]{:S(2)}) async-start(), calls=%async_computation.4 | async-start | bytes 5406720 | tf_op jit(solution)/shard_map/all_gather | solution.py:123
  18.8 15.9 %copy-start.9 = (s32[1,8]{1,0:T(1,128)S(1)}, s32[1,8]{1,0:T(1,128)}, u32[]{:S(2)}) copy-start(s32[1,8]{1,0:T(1,128)} %param.14) | copy-start | bytes 100
  18.8 16.1 %copy-start.5 = (f32[16,2048]{1,0:T(8,128)S(1)}, f32[16,2048]{1,0:T(8,128)}, u32[]{:S(2)}) copy-start(f32[16,2048]{1,0:T(8,128)} %param.22) | copy-start | bytes 393220
  22.6 27.7 %all-to-all-start = ((bf16[32,2,6144]{2,1,0:T(2,128)(2,1)}), bf16[32,2,6144]{2,1,0:T(2,128)(2,1)S(1)}, u32[]{:S(2)}, u32[]{:S(2)}) async-start(bf16[32,2,6144]{2,1,0:T(2,128)(2,1)} %reshape.221), calls=%async_computation | async-start | bytes 1572864 | tf_op jit(solution)/shard_map/all_to_all | solution.py:106
  33.1 465.6 %reduce-scatter.3.cloned.1.call-start = ((), (), s32[]{:S(2)}) async-start(), calls=%async_computation.5 | async-start | bytes 5406720 | tf_op jit(solution)/shard_map/reduce_scatter | solution.py:152
  56.9 22.1 %collective-permute-start = (bf16[3,2048,64]{1,2,0:T(8,128)(2,1)S(1)}, bf16[3,2048,64]{1,2,0:T(8,128)(2,1)S(1)}, u32[]{:S(2)}, u32[]{:S(2)}) collective-permute-start(bf16[3,2048,64]{1,2,0:T(8,128)(2,1)S(1)} %all_to_all.27), channel_id=1, source_target_pairs={{0,1},{1,0},{2,3},{3,2},{4,5},{5,4},{6,7},{7,6},{8,9},{9,8},{10,11... | collective-permute-start | bytes 2359304 | tf_op jit(solution)/shard_map/ppermute | solution.py:19
  78.9 0.9 copy-start.8
  300.8 1.0 copy-start.2
  300.8 1.2 copy-start.3
  300.8 199.0 %copy-start.1 = (bf16[40,2048]{1,0:T(8,128)(2,1)S(1)}, bf16[40,2048]{1,0:T(8,128)(2,1)}, u32[]{:S(2)}) copy-start(bf16[40,2048]{1,0:T(8,128)(2,1)} %param.13) | copy-start | bytes 491524
  300.8 199.0 %copy-start.6 = (f32[2048]{0:T(1024)S(1)}, f32[2048]{0:T(1024)}, u32[]{:S(2)}) copy-start(f32[2048]{0:T(1024)} %param.17) | copy-start | bytes 24580
  300.8 200.8 %all-gather.11.cloned.1.call-start = ((), (), s32[]{:S(2)}) async-start(), calls=%async_computation.7 | async-start | bytes 2621440 | tf_op jit(solution)/shard_map/all_gather | solution.py:101
  302.9 291.0 %all-gather.9.cloned.1.call-start = ((), (), s32[]{:S(2)}) async-start(), calls=%async_computation.6 | async-start | bytes 5406720 | tf_op jit(solution)/shard_map/all_gather | solution.py:162
  521.0 5.0 copy-start.4
  521.0 29.0 %all-to-all-start.1 = ((bf16[32,2,16384]{2,1,0:T(2,128)(2,1)}), bf16[32,2,16384]{2,1,0:T(2,128)(2,1)S(1)}, u32[]{:S(2)}, u32[]{:S(2)}) async-start(bf16[32,2,16384]{2,1,0:T(2,128)(2,1)} %reshape.223), calls=%async_computation.2 | async-start | bytes 4194304 | tf_op jit(solution)/shard_map/all_to_all | solution.py:107
  525.9 87.3 %all-gather.13.cloned.1.call-start = ((), (), s32[]{:S(2)}) async-start(), calls=%async_computation.9 | async-start | bytes 1310720 | tf_op jit(solution)/shard_map/all_gather | solution.py:102
  526.7 288.8 %reduce-scatter.5.cloned.1.call-start = ((), (), s32[]{:S(2)}) async-start(), calls=%async_computation.8 | async-start | bytes 5406720 | tf_op jit(solution)/shard_map/reduce_scatter | solution.py:170
  619.1 197.6 %copy-start = (bf16[40,2048]{1,0:T(8,128)(2,1)S(1)}, bf16[40,2048]{1,0:T(8,128)(2,1)}, u32[]{:S(2)}) copy-start(bf16[40,2048]{1,0:T(8,128)(2,1)} %fusion.33) | copy-start | bytes 491524
  619.1 197.6 %copy-start.7 = (f32[2048]{0:T(1024)S(1)}, f32[2048]{0:T(1024)}, u32[]{:S(2)}) copy-start(f32[2048]{0:T(1024)} %param.18) | copy-start | bytes 24580
Sparse Core Ops, SparseCore 0:
  11.3 93.0 all-gather.6
  300.9 197.7 reduce-scatter.2
Sparse Core Ops, SparseCore 1:
  303.0 30.8 all-gather.10
  501.6 92.2 all-gather.8
  595.4 17.7 all-gather.12
  619.2 196.3 reduce-scatter.4
where the time goes:
time: 827 us; the launch traced here: 826 us
  waiting for transfers between devices  508 us (61%)
  blocking collectives  196 us (24%)
  local copies, waits for them, and re-layouts  52.2 us (6%)
  matrix products  24.7 us (3%)
  starting transfers between devices  16.9 us (2%)
  between operations  15.4 us (2%)
  other arithmetic  12.3 us (1%)
    reduce_scatter x1, waiting for transfers between devices, per_device(): lax.psum_scatter(jnp.dot(rows_part, down_block, preferred_element_type=jn...  196 us
    reduce_scatter x1, waiting for transfers between devices, per_device(): lax.psum_scatter(jnp.dot(rows_part, output_block, preferred_element_type=...  196 us
    psum x1, blocking collectives, per_device(): query_total, key_total = lax.psum((query_sq, key_sq), 'mp')  182 us
    all_gather x1, waiting for transfers between devices, per_device(): lax.all_gather(hidden, 'mp', axis=0, tiled=True)  32.2 us
    all_gather x1, waiting for transfers between devices, per_device(): lax.all_gather(tokens, 'mp', axis=0, tiled=True)  24.5 us
    all_to_all x1, waiting for transfers between devices, per_device(): lax.all_to_all(mlp_rows, 'mp', split_axis=2, concat_axis=1, tiled=True)  22.9 us
    ppermute x1, waiting for transfers between devices, partner_2(): return lax.ppermute(block, axis, route)  20.9 us
    unnamed x24, local copies, waits for them, and re-layouts  19.6 us
  transfers between devices with their start and end apart: 9, of which 8 were waited for; matrix products, arithmetic and copies ran while one was open for 7% of the time, Pallas kernels for 0%

commit v1 on v0

--- a/solution.py
+++ b/solution.py
@@ -7,6 +7,12 @@
 HEAD_DIM = 128
 NORM_EPSILON = 1e-06
 ROPE_BASE = 500000.0
+
+
+def serve_matrix_over_axis(block_here):
+    big = jnp.stack(jnp.split(block_here, lax.psum(1, "mp"), axis=2), axis=0)
+    f_next = lax.all_to_all(big, "mp", 0, 0)
+    return jnp.concatenate(f_next, axis=1)
 
 
 def partner_2(block, axis, apart):
@@ -103,7 +109,7 @@
         lax.all_gather(output_piece, "group", axis=1, tiled=True),
     )
     attn_block, mlp_block = (
-        lax.all_to_all(attn_rows, "mp", split_axis=2, concat_axis=1, tiled=True),
+        serve_matrix_over_axis(attn_rows),
         lax.all_to_all(mlp_rows, "mp", split_axis=2, concat_axis=1, tiled=True),
     )
     down_block = down_rows[0]

time: 827 us -> 826 us (level)
    unnamed x24 -> x57, local copies, waits for them, and re-layouts: 19.6 us -> 20.7 us
where the time goes in v1:
time: 826 us; the launch traced here: 825 us
  waiting for transfers between devices  511 us (62%)
  blocking collectives  194 us (23%)
  local copies, waits for them, and re-layouts  49.4 us (6%)
  matrix products  25.2 us (3%)
  starting transfers between devices  17.4 us (2%)
  between operations  15.4 us (2%)
  other arithmetic  12.3 us (1%)
    reduce_scatter x1, waiting for transfers between devices, per_device(): lax.psum_scatter(jnp.dot(rows_part, down_block, preferred_element_type=jn...  197 us
    reduce_scatter x1, waiting for transfers between devices, per_device(): lax.psum_scatter(jnp.dot(rows_part, output_block, preferred_element_type=...  196 us
    psum x1, blocking collectives, per_device(): query_total, key_total = lax.psum((query_sq, key_sq), 'mp')  179 us
    all_gather x1, waiting for transfers between devices, per_device(): lax.all_gather(hidden, 'mp', axis=0, tiled=True)  31 us
    all_gather x1, waiting for transfers between devices, per_device(): lax.all_gather(tokens, 'mp', axis=0, tiled=True)  28.9 us
    all_to_all x1, waiting for transfers between devices, per_device(): lax.all_to_all(mlp_rows, 'mp', split_axis=2, concat_axis=1, tiled=True)  23.3 us
    unnamed x57, local copies, waits for them, and re-layouts  20.7 us
    ppermute x1, waiting for transfers between devices, partner_2(): return lax.ppermute(block, axis, route)  18.7 us
  transfers between devices with their start and end apart: 9, of which 8 were waited for; matrix products, arithmetic and copies ran while one was open for 7% of the time, Pallas kernels for 0%

profile of v1, /device:TPU:0, one launch (start us, length us, event | category | flops | bytes accessed | tf_op | source)
XLA Modules:
  0.0 824.6 jit_solution(5793490338654956942)
XLA Ops:
  10.0 8.8 %all_gather.18 = bf16[3,64,2048]{2,1,0:T(8,128)(2,1)S(1)} all-gather(bf16[3,16,2048]{2,1,0:T(8,128)(2,1)S(1)} %pad_maximum_fusion.1), channel_id=1, replica_groups=mesh['group'=4,'mp'=32] {'group'}, dimensions={1}, use_global_device_ids=true | all-gather | bytes 983040 | tf_op jit(solution)/shard_map/all_gather | solution.py:106
  20.8 1.9 reshape.229
  22.7 10.5 %all-to-all-start = ((bf16[32,2,6144]{2,1,0:T(2,128)(2,1)}), bf16[32,2,6144]{2,1,0:T(2,128)(2,1)S(1)}, u32[]{:S(2)}, u32[]{:S(2)}) async-start(bf16[32,2,6144]{2,1,0:T(2,128)(2,1)} %reshape.229), calls=%async_computation | async-start | bytes 1572864 | tf_op jit(solution)/shard_map/all_to_all | solution.py:14
  35.1 7.1 gather_fusion
  42.2 5.8 all-gather
  48.0 2.3 all-to-all-done
  51.4 1.4 copy.29
  52.8 1.3 reshape.214
  55.3 18.7 %collective-permute-done = bf16[3,2048,64]{1,2,0:T(8,128)(2,1)S(1)} collective-permute-done((bf16[3,2048,64]{1,2,0:T(8,128)(2,1)S(1)}, bf16[3,2048,64]{1,2,0:T(8,128)(2,1)S(1)}, u32[]{:S(2)}, u32[]{:S(2)}) %collective-permute-start) | collective-permute-done | bytes 786464 | tf_op jit(solution)/shard_map/ppermute | solution.py:25
  74.9 28.9 %all-gather.7.cloned.1.call-done = bf16[1280,2048]{1,0:T(8,128)(2,1)} async-done(((bf16[40,2048]{1,0:T(8,128)(2,1)}), bf16[1280,2048]{1,0:T(8,128)(2,1)}) %all-gather.7.cloned.1.call-update) | async-done | bytes 5242896 | tf_op jit(solution)/shard_map/all_gather | solution.py:129
  103.8 5.7 fusion.6
  109.6 179.4 %all-reduce = (f32[1280]{0:T(1024)S(1)}, f32[1280]{0:T(1024)S(1)}) all-reduce(f32[1280]{0:T(1024)S(1)} %broadcast_multiply_fusion.1, f32[1280]{0:T(1024)S(1)} %broadcast_multiply_fusion), channel_id=1, replica_groups=mesh['group'=4,'mp'=32] {'mp'}, use_global_device_ids=true, to_apply=%region_3.4 | all-reduce | flops 2560 | bytes 20480 | tf_op jit(solution)/shard_map/psum | solution.py:135
  289.2 1.5 fusion.55
  290.7 1.5 fusion.66
  293.2 1.3 fusion.5
  294.5 3.9 convolution_convert_fusion.1
  300.6 196.5 %reduce-scatter.3.cloned.1.call-done = bf16[40,2048]{1,0:T(8,128)(2,1)} async-done(((bf16[1280,2048]{1,0:T(8,128)(2,1)}), bf16[40,2048]{1,0:T(8,128)(2,1)}) %reduce-scatter.3.cloned.1.call-update) | async-done | bytes 163856 | tf_op jit(solution)/shard_map/reduce_scatter | solution.py:158
  497.1 1.1 fusion.30
  498.2 1.7 fusion.33
  499.9 9.5 %copy.30 = bf16[2,64,8192]{1,0,2:T(2,128)(2,1)} copy(bf16[2,64,8192]{2,1,0:T(8,128)(2,1)} %all-gather.11.cloned.1.call-done) | data formatting | bytes 4194304 | tf_op jit(solution)/shard_map/all_gather | solution.py:107
  509.5 9.8 %reshape.231 = bf16[32,2,16384]{2,1,0:T(2,128)(2,1)} reshape(bf16[8192,2,64]{2,1,0:T(2,128)(2,1)} %bitcast.178) | data formatting | bytes 4194304
  519.3 5.5 all-to-all-start.1
  525.9 23.3 %all-to-all-done.1 = bf16[32,2,16384]{2,1,0:T(2,128)(2,1)S(1)} async-done(((bf16[32,2,16384]{2,1,0:T(2,128)(2,1)}), bf16[32,2,16384]{2,1,0:T(2,128)(2,1)S(1)}, u32[]{:S(2)}, u32[]{:S(2)}) %all-to-all-start.1) | async-done | bytes 2097184 | tf_op jit(solution)/shard_map/all_to_all | solution.py:113
  549.1 4.0 reshape.232
  553.2 6.4 copy.34
  560.9 31.0 %all-gather.9.cloned.1.call-done = bf16[1280,2048]{1,0:T(8,128)(2,1)} async-done(((bf16[40,2048]{1,0:T(8,128)(2,1)}), bf16[1280,2048]{1,0:T(8,128)(2,1)}) %all-gather.9.cloned.1.call-update) | async-done | bytes 5242896 | tf_op jit(solution)/shard_map/all_gather | solution.py:168
  592.0 6.9 fusion.9
  598.8 12.4 %all-gather.13.cloned.1.call-done = bf16[256,2048]{1,0:T(8,128)(2,1)} async-done(((bf16[64,2048]{1,0:T(8,128)(2,1)}), bf16[256,2048]{1,0:T(8,128)(2,1)}) %all-gather.13.cloned.1.call-update) | async-done | bytes 1048592 | tf_op jit(solution)/shard_map/all_gather | solution.py:108
  611.3 5.9 convolution_convert_fusion
  617.2 197.0 %reduce-scatter.5.cloned.1.call-done = bf16[40,2048]{1,0:T(8,128)(2,1)} async-done(((bf16[1280,2048]{1,0:T(8,128)(2,1)}), bf16[40,2048]{1,0:T(8,128)(2,1)}) %reduce-scatter.5.cloned.1.call-update) | async-done | bytes 163856 | tf_op jit(solution)/shard_map/reduce_scatter | solution.py:176
  814.2 1.1 fusion.34
  815.3 1.7 fusion.37
  (99 shorter events, 15.5 us)
Async XLA Ops:
  7.4 96.4 %all-gather.7.cloned.1.call-start = ((), (), s32[]{:S(2)}) async-start(), calls=%async_computation.4 | async-start | bytes 5406720 | tf_op jit(solution)/shard_map/all_gather | solution.py:129
  20.8 14.0 %copy-start.10 = (s32[1,8]{1,0:T(1,128)S(1)}, s32[1,8]{1,0:T(1,128)}, u32[]{:S(2)}) copy-start(s32[1,8]{1,0:T(1,128)} %param.14) | copy-start | bytes 100
  20.8 14.2 %copy-start.6 = (f32[16,2048]{1,0:T(8,128)S(1)}, f32[16,2048]{1,0:T(8,128)}, u32[]{:S(2)}) copy-start(f32[16,2048]{1,0:T(8,128)} %param.22) | copy-start | bytes 393220
  22.7 27.7 %all-to-all-start = ((bf16[32,2,6144]{2,1,0:T(2,128)(2,1)}), bf16[32,2,6144]{2,1,0:T(2,128)(2,1)S(1)}, u32[]{:S(2)}, u32[]{:S(2)}) async-start(bf16[32,2,6144]{2,1,0:T(2,128)(2,1)} %reshape.229), calls=%async_computation | async-start | bytes 1572864 | tf_op jit(solution)/shard_map/all_to_all | solution.py:14
  33.2 463.9 %reduce-scatter.3.cloned.1.call-start = ((), (), s32[]{:S(2)}) async-start(), calls=%async_computation.5 | async-start | bytes 5406720 | tf_op jit(solution)/shard_map/reduce_scatter | solution.py:158
  54.1 19.9 %copy-start.1 = (bf16[3,2048,64]{1,2,0:T(8,128)(2,1)}, bf16[3,2048,64]{1,2,0:T(8,128)(2,1)S(1)}, u32[]{:S(2)}) copy-start(bf16[3,2048,64]{1,2,0:T(8,128)(2,1)S(1)} %reshape.214) | copy-start | bytes 2359300
  54.1 19.9 %collective-permute-start = (bf16[3,2048,64]{1,2,0:T(8,128)(2,1)S(1)}, bf16[3,2048,64]{1,2,0:T(8,128)(2,1)S(1)}, u32[]{:S(2)}, u32[]{:S(2)}) collective-permute-start(bf16[3,2048,64]{1,2,0:T(8,128)(2,1)S(1)} %reshape.214), channel_id=1, source_target_pairs={{0,1},{1,0},{2,3},{3,2},{4,5},{5,4},{6,7},{7,6},{8,9},{9,8},{10,11... | collective-permute-start | bytes 2359304 | tf_op jit(solution)/shard_map/ppermute | solution.py:25
  74.0 0.9 copy-start.9
  298.4 1.0 copy-start.3
  298.4 1.2 copy-start.4
  298.4 199.7 %copy-start.2 = (bf16[40,2048]{1,0:T(8,128)(2,1)S(1)}, bf16[40,2048]{1,0:T(8,128)(2,1)}, u32[]{:S(2)}) copy-start(bf16[40,2048]{1,0:T(8,128)(2,1)} %param.13) | copy-start | bytes 491524
  298.4 199.7 %copy-start.7 = (f32[2048]{0:T(1024)S(1)}, f32[2048]{0:T(1024)}, u32[]{:S(2)}) copy-start(f32[2048]{0:T(1024)} %param.17) | copy-start | bytes 24580
  298.5 201.5 %all-gather.11.cloned.1.call-start = ((), (), s32[]{:S(2)}) async-start(), calls=%async_computation.7 | async-start | bytes 2621440 | tf_op jit(solution)/shard_map/all_gather | solution.py:107
  300.5 291.4 %all-gather.9.cloned.1.call-start = ((), (), s32[]{:S(2)}) async-start(), calls=%async_computation.6 | async-start | bytes 5406720 | tf_op jit(solution)/shard_map/all_gather | solution.py:168
  519.3 5.5 copy-start.5
  519.3 29.8 %all-to-all-start.1 = ((bf16[32,2,16384]{2,1,0:T(2,128)(2,1)}), bf16[32,2,16384]{2,1,0:T(2,128)(2,1)S(1)}, u32[]{:S(2)}, u32[]{:S(2)}) async-start(bf16[32,2,16384]{2,1,0:T(2,128)(2,1)} %reshape.231), calls=%async_computation.2 | async-start | bytes 4194304 | tf_op jit(solution)/shard_map/all_to_all | solution.py:113
  524.8 86.5 %all-gather.13.cloned.1.call-start = ((), (), s32[]{:S(2)}) async-start(), calls=%async_computation.9 | async-start | bytes 1310720 | tf_op jit(solution)/shard_map/all_gather | solution.py:108
  525.6 288.6 %reduce-scatter.5.cloned.1.call-start = ((), (), s32[]{:S(2)}) async-start(), calls=%async_computation.8 | async-start | bytes 5406720 | tf_op jit(solution)/shard_map/reduce_scatter | solution.py:176
  617.2 198.1 %copy-start = (bf16[40,2048]{1,0:T(8,128)(2,1)S(1)}, bf16[40,2048]{1,0:T(8,128)(2,1)}, u32[]{:S(2)}) copy-start(bf16[40,2048]{1,0:T(8,128)(2,1)} %fusion.33) | copy-start | bytes 491524
  617.2 198.1 %copy-start.8 = (f32[2048]{0:T(1024)S(1)}, f32[2048]{0:T(1024)}, u32[]{:S(2)}) copy-start(f32[2048]{0:T(1024)} %param.18) | copy-start | bytes 24580
Sparse Core Ops, SparseCore 0:
  11.3 92.4 all-gather.6
  298.6 198.4 reduce-scatter.2
Sparse Core Ops, SparseCore 1:
  300.6 31.5 all-gather.10
  500.0 91.9 all-gather.8
  593.5 17.7 all-gather.12
  617.3 196.9 reduce-scatter.4
